TPU v7x, 32 devices: a whole 2x2x4 slice. The times are simulated.
32 devices in a mesh: row: 16 (over z, y, core), col: 2 (over x).
Axes of the slice: x: 2, y: 2, z: 4, core: 2. Of those that a mesh axis runs over, the one named last changes fastest.
Arguments:
- jacobian: bfloat16 [512, 256, 128], P(('col', 'row')), may hold values from -1.5 to 1.5
- weights: bfloat16 [32, 512, 256], P('row', 'col'), may hold values from 0.25 to 4
- panel_weights: bfloat16 [512, 256], P(('col', 'row')), may hold values from 0.25 to 4
- damping: float32 [32, 128], P('row'), may hold values from 0.01 to 1
- panel_inverse: float32 [128, 128], replicated, may hold values from -0.12 to 0.12
Outputs:
- schur: float32 [4096, 65536], P('row', 'col')
All inputs are finite; a program needn't handle non-finite values.
Results may differ from a plain program's by a relative error of at most 0.0022.
Values may be sent and summed in bfloat16 or wider, within the bound.
No kernel may reach another device: no remote copies, remote signals or barrier semaphores. Data moves between devices by JAX's collectives and lax.ppermute only.
A program may use at most 128 MiB of HBM per device.

v0:
```python
import jax
import jax.numpy as jnp
from jax import lax
from jax.sharding import PartitionSpec as P

HIGHEST = lax.Precision.HIGHEST


def broadcast(value, axis, root):
    mine = lax.axis_index(axis) == root
    return lax.psum(jnp.where(mine, value, jnp.zeros_like(value)), axis)


def shards(jacobian, weights, panel_weights, damping, panel_inverse):
    per_dev, sample_rows, param_width = jacobian.shape
    slab_rows, col_block, _ = weights.shape
    row_count = lax.axis_size("row")
    col_count = lax.axis_size("col")
    row_index = lax.axis_index("row")
    col_index = lax.axis_index("col")
    station_total = col_block * col_count
    panel_id = station_total - 1
    slab_ids = row_index * slab_rows + jnp.arange(slab_rows, dtype=jnp.int32)
    col_base = col_index * col_block
    col_ids = col_base + jnp.arange(col_block, dtype=jnp.int32)
    station_piece = lax.all_gather(jacobian, "row", axis=0, tiled=True)
    how_many = station_piece.shape[0]
    piece_ids = col_base + jnp.arange(how_many, dtype=jnp.int32)
    self_pair = slab_ids[:, None] == piece_ids[None, :]
    scaled = weights.astype(jnp.float32)[..., None] * station_piece.astype(jnp.float32)[None]
    scaled = jnp.where(self_pair[:, :, None, None], 0.0, scaled).astype(jnp.bfloat16)
    gram_part = jnp.einsum(
        "ijra,jrb->iab", scaled, station_piece, preferred_element_type=jnp.float32
    )
    gathered = station_piece
    scaled_all = scaled
    gram_part, gathered, scaled_all = (gram_part, gathered, scaled_all)
    home_col = row_index * slab_rows // col_block
    offset = row_index * slab_rows % col_block
    my_slab = lax.dynamic_slice_in_dim(gathered, offset, slab_rows, 0)
    slab_jac = broadcast(my_slab, "col", home_col)
    coupling = jnp.einsum(
        "ijra,irb->iajb", scaled_all, slab_jac, preferred_element_type=jnp.float32
    )
    gram_sum = lax.psum(gram_part, "col")
    identity = jnp.eye(param_width, dtype=jnp.float32)
    diag_block = (
        gram_sum + identity[None] * (jnp.diagonal(gram_sum, axis1=1, axis2=2) * damping)[:, None, :]
    )
    on_self = slab_ids[:, None] == col_ids[None, :]
    hessian = jnp.where(on_self[:, None, :, None], diag_block[:, :, None, :], coupling)
    local_factor = jnp.einsum(
        "iac,cb->iab",
        hessian[:, :, col_block - 1, :],
        panel_inverse,
        precision=HIGHEST,
        preferred_element_type=jnp.float32,
    )
    panel_factor, panel_jac = (
        broadcast(local_factor.astype(jnp.bfloat16), "col", col_count - 1).astype(
            local_factor.dtype
        ),
        broadcast(gathered[col_block - 1], "col", col_count - 1),
    )
    own_ids = (col_index * row_count + row_index) * per_dev + jnp.arange(per_dev, dtype=jnp.int32)
    scaled_rows = panel_weights.astype(jnp.float32)[..., None] * jacobian.astype(jnp.float32)
    scaled_rows = jnp.where((own_ids == panel_id)[:, None, None], 0.0, scaled_rows).astype(
        jnp.bfloat16
    )
    row_part = jnp.einsum("jra,rb->jab", scaled_rows, panel_jac, preferred_element_type=jnp.float32)
    station_piece = lax.all_gather(row_part.astype(jnp.bfloat16), "row", axis=0, tiled=True).astype(
        jnp.float32
    )
    how_many = station_piece.shape[0]
    current = lax.slice_in_dim(hessian, 0, how_many, axis=2)
    correction = jnp.einsum(
        "iac,jcb->iajb",
        panel_factor,
        station_piece,
        precision=HIGHEST,
        preferred_element_type=jnp.float32,
    )
    piece_ids = col_base + jnp.arange(how_many, dtype=jnp.int32)
    result = jnp.where(
        (piece_ids == panel_id)[None, None, :, None],
        panel_factor[:, :, None, :],
        current - correction,
    )
    return result.reshape(slab_rows * param_width, how_many * param_width)


def solution(mesh):
    return jax.shard_map(
        shards,
        mesh=mesh,
        in_specs=(
            P(("col", "row"), None, None),
            P("row", "col", None),
            P(("col", "row"), None),
            P("row", None),
            P(),
        ),
        out_specs=P("row", "col"),
        check_vma=False,
    )
```

profile of v0, /device:TPU:0, one launch (start us, length us, event | category | flops | bytes accessed | tf_op | source)
XLA Modules:
  0.0 486.4 jit_solution(10741653485367392175)
XLA Ops:
  6.5 0.0 copy-start
  6.5 0.0 all-gather.3.cloned.1.call-start
  6.5 0.7 all-gather.3.cloned.1.call-update
  7.3 0.0 all-reduce.5.cloned.1.call-start
  7.3 1.0 convert_element_type.35
  8.4 0.1 broadcast_compare_fusion
  8.5 130.7 %all-gather.3.cloned.1.call-done = bf16[256,256,128]{2,1,0:T(8,128)(2,1)} async-done(((bf16[16,256,128]{2,1,0:T(8,128)(2,1)}), bf16[256,256,128]{2,1,0:T(8,128)(2,1)}) %all-gather.3.cloned.1.call-update) | async-done | bytes 16777232 | tf_op jit(solution)/shard_map/all_gather | solution.py:26
  139.1 0.9 constant_dynamic-slice_fusion
  140.1 0.1 copy.53
  140.2 9.4 %convert_element_type.36 = f32[256,256,128]{2,1,0:T(8,128)S(1)} convert(bf16[256,256,128]{2,1,0:T(8,128)(2,1)} %all-gather.3.cloned.1.call-done) | non-fusion elementwise | flops 8388608 | bytes 50331648 | tf_op jit(solution)/shard_map/convert_element_type | solution.py:30
  149.6 0.0 copy-start.1
  149.6 11.7 %copy-done.1 = f32[256,256,128]{2,1,0:T(8,128)} copy-done((f32[256,256,128]{2,1,0:T(8,128)}, f32[256,256,128]{2,1,0:T(8,128)S(1)}, u32[]{:S(2)}) %copy-start.1) | copy-done | bytes 33554456
  161.3 0.0 copy-start.5
  161.3 47.9 %fusion.12 = f32[2,128,128]{2,1,0:T(8,128)} fusion(bf16[256,256,128]{2,1,0:T(8,128)(2,1)} %all-gather.3.cloned.1.call-done, f32[256,256,128]{2,1,0:T(8,128)S(1)} %convert_element_type.36, f32[2,256,256]{2,1,0:T(8,128)S(1)} %convert_element_type.35, pred[2,256]{1,0:T(4,128)(4,1)S(1)} %broadcast_compare_fusion), kind=kOutput, calls=%fused_computation.19 | convolution fusion | flops 4345298944 | bytes 50987520 | tf_op jit(solution)/shard_map/ijra,jrb->iab/dot_general | solution.py:32
  209.2 0.0 all-reduce.5.cloned.1.call-update
  209.2 0.0 all-reduce.7.cloned.1.call-start
  209.2 0.7 broadcast_select_fusion
  209.9 0.0 all-reduce.7.cloned.1.call-update
  209.9 0.0 all-reduce.9.cloned.1.call-start
  210.0 1.5 fusion.20
  211.5 17.5 %all-reduce.5.cloned.1.call-done = f32[2,128,128]{2,1,0:T(8,128)} async-done(((f32[2,128,128]{2,1,0:T(8,128)}), f32[2,128,128]{2,1,0:T(8,128)}) %all-reduce.5.cloned.1.call-update) | async-done | bytes 131088 | tf_op jit(solution)/shard_map/psum | solution.py:45
  228.9 5.5 %copy.37 = f32[2,128,128]{0,2,1:T(8,128)} copy(f32[2,128,128]{2,1,0:T(8,128)} %all-reduce.5.cloned.1.call-done) | data formatting | bytes 262144 | tf_op jit(solution)/shard_map/psum | solution.py:45
  234.4 1.8 gather_fusion
  236.2 0.1 copy.38
  236.3 0.0 copy-done.5
  236.3 0.9 multiply_add_fusion
  237.2 0.1 copy.39
  237.3 0.0 copy-start.4
  237.3 0.0 copy-start.3
  237.4 15.3 %all-reduce.7.cloned.1.call-done = bf16[2,256,128]{1,2,0:T(8,128)(2,1)} async-done(((bf16[2,256,128]{1,2,0:T(8,128)(2,1)}), bf16[2,256,128]{1,2,0:T(8,128)(2,1)}) %all-reduce.7.cloned.1.call-update) | async-done | bytes 131088 | tf_op jit(solution)/shard_map/psum | solution.py:11
  252.7 23.6 %bitcast_select_fusion = f32[2,128,256,128]{1,3,2,0:T(8,128)S(1)} fusion(f32[2,128,128]{1,2,0:T(8,128)S(1)} %copy.39, pred[2,256]{1,0:T(4,128)(4,1)S(1)} %broadcast_compare_fusion, f32[256,256,128]{2,1,0:T(8,128)} %copy-done.1, f32[2,256,256]{2,1,0:T(8,128)S(1)} %convert_element_type.35, bf16[2,256,128]{1,2,0:T(8,128)(2,1)} %all-reduce.7.cloned.1.call-done), kind=kOutput, calls=%fused_computation.5 | convolution fusion | flops 4353687552 | bytes 67895808 | tf_op jit(solution)/shard_map/ijra,irb->iajb/dot_general | solution.py:42
  276.3 0.0 copy-start.2
  276.3 11.7 %copy-done.2 = f32[2,128,256,128]{1,3,2,0:T(8,128)} copy-done((f32[2,128,256,128]{1,3,2,0:T(8,128)}, f32[2,128,256,128]{1,3,2,0:T(8,128)S(1)}, u32[]{:S(2)}) %copy-start.2) | copy-done | bytes 33554456
  288.0 0.0 copy-done
  288.0 1.0 fusion.15
  289.0 0.0 all-reduce.9.cloned.1.call-update
  289.1 0.2 all-gather.5.cloned.1.call-start
  289.3 0.0 copy-done.4
  289.3 21.5 %all-reduce.9.cloned.1.call-done = (bf16[2,128,128]{2,1,0:T(8,128)(2,1)}, bf16[256,128]{1,0:T(8,128)(2,1)}) async-done(((bf16[2,128,128]{2,1,0:T(8,128)(2,1)}, bf16[256,128]{1,0:T(8,128)(2,1)}), (bf16[2,128,128]{2,1,0:T(8,128)(2,1)}, bf16[256,128]{1,0:T(8,128)(2,1)})) %all-reduce.9.cloned.1.call-update) | async-done | bytes 131088 | tf_op jit(solution)/shard_map/psum | solution.py:11
  310.8 0.0 copy-done.3
  310.8 2.9 convolution_convert_fusion
  313.7 0.0 all-gather.5.cloned.1.call-update
  313.7 0.9 copy.42
  314.7 74.1 %all-gather.5.cloned.1.call-done = bf16[256,128,128]{2,1,0:T(8,128)(2,1)} async-done(((bf16[16,128,128]{2,1,0:T(8,128)(2,1)}), bf16[256,128,128]{2,1,0:T(8,128)(2,1)}) %all-gather.5.cloned.1.call-update) | async-done | bytes 8388624 | tf_op jit(solution)/shard_map/all_gather | solution.py:71
  388.8 28.2 %subtract_select_fusion = f32[2,128,256,128]{1,3,2,0:T(8,128)} fusion(f32[2,128,256,128]{1,3,2,0:T(8,128)} %copy-done.2, f32[2,128,128]{1,2,0:T(8,128)S(1)} %copy.42, pred[256]{0:T(512)(128)(4,1)S(1)} %broadcast_compare_fusion.1, bf16[256,128,128]{2,1,0:T(8,128)(2,1)} %all-gather.5.cloned.1.call-done, bf16[2,128,128]{2,1,0:T(8,128)(2,1)} %get-tuple-element.5), kind=kOutput, calls=%fused_computation.6 | convolution fusion | flops 2164260864 | bytes 75694336 | tf_op jit(solution)/shard_map/iac,jcb->iajb/dot_general | solution.py:76
  417.0 31.1 %copy.45 = f32[2,128,256,128]{3,2,1,0:T(8,128)} copy(f32[2,128,256,128]{1,3,2,0:T(8,128)} %subtract_select_fusion) | data formatting | bytes 67108864 | tf_op jit(solution)/shard_map/jit(_where)/select_n | solution.py:84
  448.1 31.8 %copy.56 = f32[32,8,256,128]{3,1,2,0:T(8,128)} copy(f32[32,8,256,128]{3,2,1,0:T(8,128)} %bitcast.47) | data formatting | bytes 67108864
  (8 shorter events, 0.1 us)
Async XLA Ops:
  6.5 281.5 %copy-start = (f32[128,128]{1,0:T(8,128)S(1)}, f32[128,128]{1,0:T(8,128)}, u32[]{:S(2)}) copy-start(f32[128,128]{1,0:T(8,128)} %param.9) | copy-start | bytes 196612
  6.5 132.6 %all-gather.3.cloned.1.call-start = ((), (), s32[]{:S(2)}) async-start(), calls=%async_computation | async-start | bytes 17825792 | tf_op jit(solution)/shard_map/all_gather | solution.py:26
  7.3 221.7 %all-reduce.5.cloned.1.call-start = ((), (), s32[]{:S(2)}) async-start(), calls=%async_computation.1 | async-start | bytes 262144 | tf_op jit(solution)/shard_map/psum | solution.py:45
  149.6 11.7 %copy-start.1 = (f32[256,256,128]{2,1,0:T(8,128)}, f32[256,256,128]{2,1,0:T(8,128)S(1)}, u32[]{:S(2)}) copy-start(f32[256,256,128]{2,1,0:T(8,128)S(1)} %convert_element_type.36) | copy-start | bytes 100663296
  161.3 75.0 %copy-start.5 = (f32[2,128]{1,0:T(2,128)S(1)}, f32[2,128]{1,0:T(2,128)}, u32[]{:S(2)}) copy-start(f32[2,128]{1,0:T(2,128)} %param.8) | copy-start | bytes 3076
  209.2 43.5 %all-reduce.7.cloned.1.call-start = ((), (), s32[]{:S(2)}) async-start(), calls=%async_computation.2 | async-start | bytes 262144 | tf_op jit(solution)/shard_map/psum | solution.py:11
  209.9 100.9 %all-reduce.9.cloned.1.call-start = ((), (), s32[]{:S(2)}) async-start(), calls=%async_computation.4 | async-start | bytes 262144 | tf_op jit(solution)/shard_map/psum | solution.py:11
  237.3 52.0 %copy-start.4 = (bf16[16,256]{1,0:T(8,128)(2,1)S(1)}, bf16[16,256]{1,0:T(8,128)(2,1)}, u32[]{:S(2)}) copy-start(bf16[16,256]{1,0:T(8,128)(2,1)} %param.7) | copy-start | bytes 24580
  237.3 73.5 %copy-start.3 = (bf16[16,256,128]{2,1,0:T(8,128)(2,1)S(1)}, bf16[16,256,128]{2,1,0:T(8,128)(2,1)}, u32[]{:S(2)}) copy-start(bf16[16,256,128]{2,1,0:T(8,128)(2,1)} %param.5) | copy-start | bytes 3145732
  276.3 11.7 %copy-start.2 = (f32[2,128,256,128]{1,3,2,0:T(8,128)}, f32[2,128,256,128]{1,3,2,0:T(8,128)S(1)}, u32[]{:S(2)}) copy-start(f32[2,128,256,128]{1,3,2,0:T(8,128)S(1)} %bitcast_select_fusion) | copy-start | bytes 100663296
  289.1 99.7 %all-gather.5.cloned.1.call-start = ((), (), s32[]{:S(2)}) async-start(), calls=%async_computation.3 | async-start | bytes 8912896 | tf_op jit(solution)/shard_map/all_gather | solution.py:71
Sparse Core Ops, SparseCore 0:
  9.5 129.5 all-gather.2
  209.3 19.5 all-reduce.4
  231.2 21.4 all-reduce.6
  289.2 21.5 all-reduce.8
  313.8 74.8 all-gather.4
where the time goes:
time: 488 us; the launch traced here: 486 us
  waiting for transfers between devices  260 us (53%)
  matrix products  104 us (21%)
  local copies, waits for them, and re-layouts  95.7 us (20%)
  other arithmetic  13.6 us (3%)
  between operations  13.3 us (3%)
    all_gather x1, waiting for transfers between devices, shards(): station_piece = lax.all_gather(jacobian, 'row', axis=0, tiled=True)  131 us
    all_gather x1, waiting for transfers between devices, shards(): lax.all_gather(row_part.astype(jnp.bfloat16), 'row', axis=0, tiled=True)  74.1 us
    unnamed x14, local copies, waits for them, and re-layouts  55.3 us
    dot_general x1, matrix products, shards(): jnp.einsum('ijra,jrb->iab', scaled, station_piece, preferred_element_type...  47.9 us
    psum x2, waiting for transfers between devices, broadcast(): return lax.psum(jnp.where(mine, value, jnp.zeros_like(value)), axis)  36.8 us
    select_n x1, local copies, waits for them, and re-layouts, shards(): jnp.where((piece_ids == panel_id)[None, None, :, None], panel_factor[:, :...  31.1 us
    dot_general x1, matrix products, shards(): jnp.einsum('iac,jcb->iajb', panel_factor, station_piece, precision=HIGHES...  28.2 us
    dot_general x1, matrix products, shards(): jnp.einsum('ijra,irb->iajb', scaled_all, slab_jac, preferred_element_type...  23.6 us
  transfers between devices with their start and end apart: 5, of which 5 were waited for; matrix products, arithmetic and copies ran while one was open for 3% of the time, Pallas kernels for 0%

commit v1 on v0

--- a/solution.py
+++ b/solution.py
@@ -1,9 +1,18 @@
+import functools
 import jax
 import jax.numpy as jnp
 from jax import lax
 from jax.sharding import PartitionSpec as P
 
 HIGHEST = lax.Precision.HIGHEST
+
+
+def regions_save(array_here, a_name):
+    d_next = jax.lax.all_gather(array_here, a_name)
+    return jnp.sum(d_next, axis=0)
+
+
+_rest_spot = functools.partial(regions_save, a_name="col")
 
 
 def broadcast(value, axis, root):
@@ -42,7 +51,7 @@
     coupling = jnp.einsum(
         "ijra,irb->iajb", scaled_all, slab_jac, preferred_element_type=jnp.float32
     )
-    gram_sum = lax.psum(gram_part, "col")
+    gram_sum = _rest_spot(gram_part)
     identity = jnp.eye(param_width, dtype=jnp.float32)
     diag_block = (
         gram_sum + identity[None] * (jnp.diagonal(gram_sum, axis1=1, axis2=2) * damping)[:, None, :]

time: 488 us -> 445 us (0.912)
  waiting for transfers between devices: 260 us -> 225 us
  local copies, waits for them, and re-layouts: 95.7 us -> 83.2 us
  blocking collectives: 0 us -> 6.33 us
    psum x1 -> x0, waiting for transfers between devices: 17.5 us -> none  [shards(): gram_sum = lax.psum(gram_part, 'col')]
    psum x2, waiting for transfers between devices: 36.8 us -> 19.6 us  [broadcast(): return lax.psum(jnp.where(mine, value, jnp.zeros_like(value)), axis)]
    unnamed x14, local copies, waits for them, and re-layouts: 55.3 us -> 43.6 us
    all_gather x0 -> x1, blocking collectives: none -> 6.33 us  [regions_save(): d_next = jax.lax.all_gather(array_here, a_name)]
    psum x1 -> x0, local copies, waits for them, and re-layouts: 5.49 us -> none  [shards(): gram_sum = lax.psum(gram_part, 'col')]
  transfers between devices with their start and end apart: 5 -> 4, of which waited for: 5 -> 3; matrix products, arithmetic and copies ran while one was open for 3% -> 15% of each run, Pallas kernels for 0% -> 0%
where the time goes in v1:
time: 445 us; the launch traced here: 444 us
  waiting for transfers between devices  225 us (51%)
  matrix products  103 us (23%)
  local copies, waits for them, and re-layouts  83.2 us (19%)
  between operations  13.3 us (3%)
  other arithmetic  12.8 us (3%)
  blocking collectives  6.33 us (1%)
    all_gather x1, waiting for transfers between devices, shards(): station_piece = lax.all_gather(jacobian, 'row', axis=0, tiled=True)  131 us
    all_gather x1, waiting for transfers between devices, shards(): lax.all_gather(row_part.astype(jnp.bfloat16), 'row', axis=0, tiled=True)  74.1 us
    dot_general x1, matrix products, shards(): jnp.einsum('ijra,jrb->iab', scaled, station_piece, preferred_element_type...  47.4 us
    unnamed x14, local copies, waits for them, and re-layouts  43.6 us
    select_n x1, local copies, waits for them, and re-layouts, shards(): jnp.where((piece_ids == panel_id)[None, None, :, None], panel_factor[:, :...  31.2 us
    dot_general x1, matrix products, shards(): jnp.einsum('iac,jcb->iajb', panel_factor, station_piece, precision=HIGHES...  28.2 us
    dot_general x1, matrix products, shards(): jnp.einsum('ijra,irb->iajb', scaled_all, slab_jac, preferred_element_type...  23.7 us
    psum x2, waiting for transfers between devices, broadcast(): return lax.psum(jnp.where(mine, value, jnp.zeros_like(value)), axis)  19.6 us
  transfers between devices with their start and end apart: 4, of which 3 were waited for; matrix products, arithmetic and copies ran while one was open for 15% of the time, Pallas kernels for 0%

profile of v1, /device:TPU:0, one launch (start us, length us, event | category | flops | bytes accessed | tf_op | source)
XLA Modules:
  0.0 444.3 jit_solution(7773262017936105153)
XLA Ops:
  6.5 0.0 copy-start
  6.5 0.0 all-gather.4.cloned.1.call-start
  6.5 0.7 all-gather.4.cloned.1.call-update
  7.3 0.0 all-reduce.4.cloned.1.call-start
  7.3 1.0 convert_element_type.35
  8.4 0.1 broadcast_compare_fusion
  8.5 130.7 %all-gather.4.cloned.1.call-done = bf16[256,256,128]{2,1,0:T(8,128)(2,1)} async-done(((bf16[16,256,128]{2,1,0:T(8,128)(2,1)}), bf16[256,256,128]{2,1,0:T(8,128)(2,1)}) %all-gather.4.cloned.1.call-update) | async-done | bytes 16777232 | tf_op jit(solution)/shard_map/all_gather | solution.py:35
  139.1 0.9 constant_dynamic-slice_fusion
  140.1 0.1 copy.49
  140.2 0.7 broadcast_select_fusion
  140.8 0.0 all-reduce.4.cloned.1.call-update
  140.9 0.0 all-reduce.6.cloned.1.call-start
  140.9 9.5 %convert_element_type.36 = f32[256,256,128]{2,1,0:T(8,128)S(1)} convert(bf16[256,256,128]{2,1,0:T(8,128)(2,1)} %all-gather.4.cloned.1.call-done) | non-fusion elementwise | flops 8388608 | bytes 50331648 | tf_op jit(solution)/shard_map/convert_element_type | solution.py:39
  150.4 0.0 copy-start.1
  150.4 0.0 copy-start.5
  150.4 47.4 %fusion.12 = f32[2,128,128]{2,1,0:T(8,128)S(1)} fusion(bf16[256,256,128]{2,1,0:T(8,128)(2,1)} %all-gather.4.cloned.1.call-done, f32[256,256,128]{2,1,0:T(8,128)S(1)} %convert_element_type.36, f32[2,256,256]{2,1,0:T(8,128)S(1)} %convert_element_type.35, pred[2,256]{1,0:T(4,128)(4,1)S(1)} %broadcast_compare_fusion), kind=kOutput, calls=%fused_computation.19 | convolution fusion | flops 4345298944 | bytes 50987520 | tf_op jit(solution)/shard_map/ijra,jrb->iab/dot_general | solution.py:41
  197.8 0.0 copy-done.1
  197.8 6.3 %all-gather = f32[4,128,128]{2,1,0:T(8,128)S(1)} all-gather(f32[2,128,128]{2,1,0:T(8,128)S(1)} %fusion.12), channel_id=2, replica_groups=mesh['row'=16,'col'=2] {'col'}, dimensions={0}, use_global_device_ids=true | all-gather | bytes 393216 | tf_op jit(solution)/shard_map/all_gather | solution.py:11
  204.2 4.6 %copy.33 = f32[2,128,128]{0,2,1:T(8,128)} copy(f32[2,128,128]{2,1,0:T(8,128)S(1)} %reduce_sum.9) | data formatting | bytes 262144 | tf_op jit(solution)/shard_map/reduce_sum | solution.py:12
  208.8 1.8 gather_fusion
  210.6 0.1 copy.34
  210.6 0.0 copy-done.5
  210.7 0.1 copy.35
  210.8 1.5 fusion.20
  212.2 0.0 copy-start.4
  212.2 0.0 copy-start.3
  212.2 0.0 all-reduce.4.cloned.1.call-done
  212.2 23.7 %bitcast_select_fusion = f32[2,128,256,128]{1,3,2,0:T(8,128)S(1)} fusion(f32[2,128,128]{1,2,0:T(8,128)S(1)} %copy.35, pred[2,256]{1,0:T(4,128)(4,1)S(1)} %broadcast_compare_fusion, f32[256,256,128]{2,1,0:T(8,128)} %copy-done.1, f32[2,256,256]{2,1,0:T(8,128)S(1)} %convert_element_type.35, bf16[2,256,128]{1,2,0:T(8,128)(2,1)} %all-reduce.4.cloned.1.call-done), kind=kOutput, calls=%fused_computation.5 | convolution fusion | flops 4353687552 | bytes 67895808 | tf_op jit(solution)/shard_map/ijra,irb->iajb/dot_general | solution.py:51
  236.0 0.0 copy-start.2
  236.0 11.7 %copy-done.2 = f32[2,128,256,128]{1,3,2,0:T(8,128)} copy-done((f32[2,128,256,128]{1,3,2,0:T(8,128)}, f32[2,128,256,128]{1,3,2,0:T(8,128)S(1)}, u32[]{:S(2)}) %copy-start.2) | copy-done | bytes 33554456
  247.6 0.0 copy-done
  247.6 1.0 fusion.15
  248.6 0.0 all-reduce.6.cloned.1.call-update
  248.7 0.2 all-gather.6.cloned.1.call-start
  248.9 0.0 copy-done.4
  248.9 19.6 %all-reduce.6.cloned.1.call-done = (bf16[2,128,128]{2,1,0:T(8,128)(2,1)}, bf16[256,128]{1,0:T(8,128)(2,1)}) async-done(((bf16[2,128,128]{2,1,0:T(8,128)(2,1)}, bf16[256,128]{1,0:T(8,128)(2,1)}), (bf16[2,128,128]{2,1,0:T(8,128)(2,1)}, bf16[256,128]{1,0:T(8,128)(2,1)})) %all-reduce.6.cloned.1.call-update) | async-done | bytes 131088 | tf_op jit(solution)/shard_map/psum | solution.py:20
  268.6 0.0 copy-done.3
  268.6 2.9 convolution_convert_fusion
  271.5 0.0 all-gather.6.cloned.1.call-update
  271.5 0.9 copy.38
  272.5 74.1 %all-gather.6.cloned.1.call-done = bf16[256,128,128]{2,1,0:T(8,128)(2,1)} async-done(((bf16[16,128,128]{2,1,0:T(8,128)(2,1)}), bf16[256,128,128]{2,1,0:T(8,128)(2,1)}) %all-gather.6.cloned.1.call-update) | async-done | bytes 8388624 | tf_op jit(solution)/shard_map/all_gather | solution.py:80
  346.6 28.2 %subtract_select_fusion = f32[2,128,256,128]{1,3,2,0:T(8,128)} fusion(f32[2,128,256,128]{1,3,2,0:T(8,128)} %copy-done.2, f32[2,128,128]{1,2,0:T(8,128)S(1)} %copy.38, pred[256]{0:T(512)(128)(4,1)S(1)} %broadcast_compare_fusion.1, bf16[256,128,128]{2,1,0:T(8,128)(2,1)} %all-gather.6.cloned.1.call-done, bf16[2,128,128]{2,1,0:T(8,128)(2,1)} %get-tuple-element.5), kind=kOutput, calls=%fused_computation.6 | convolution fusion | flops 2164260864 | bytes 75694336 | tf_op jit(solution)/shard_map/iac,jcb->iajb/dot_general | solution.py:85
  374.8 31.2 %copy.41 = f32[2,128,256,128]{3,2,1,0:T(8,128)} copy(f32[2,128,256,128]{1,3,2,0:T(8,128)} %subtract_select_fusion) | data formatting | bytes 67108864 | tf_op jit(solution)/shard_map/jit(_where)/select_n | solution.py:93
  406.0 31.8 %copy.52 = f32[32,8,256,128]{3,1,2,0:T(8,128)} copy(f32[32,8,256,128]{3,2,1,0:T(8,128)} %bitcast.48) | data formatting | bytes 67108864
  (10 shorter events, 0.1 us)
Async XLA Ops:
  6.5 241.1 %copy-start = (f32[128,128]{1,0:T(8,128)S(1)}, f32[128,128]{1,0:T(8,128)}, u32[]{:S(2)}) copy-start(f32[128,128]{1,0:T(8,128)} %param.9) | copy-start | bytes 196612
  6.5 132.6 %all-gather.4.cloned.1.call-start = ((), (), s32[]{:S(2)}) async-start(), calls=%async_computation | async-start | bytes 17825792 | tf_op jit(solution)/shard_map/all_gather | solution.py:35
  7.3 205.0 %all-reduce.4.cloned.1.call-start = ((), (), s32[]{:S(2)}) async-start(), calls=%async_computation.1 | async-start | bytes 262144 | tf_op jit(solution)/shard_map/psum | solution.py:20
  140.9 127.7 %all-reduce.6.cloned.1.call-start = ((), (), s32[]{:S(2)}) async-start(), calls=%async_computation.3 | async-start | bytes 262144 | tf_op jit(solution)/shard_map/psum | solution.py:20
  150.4 47.4 %copy-start.1 = (f32[256,256,128]{2,1,0:T(8,128)}, f32[256,256,128]{2,1,0:T(8,128)S(1)}, u32[]{:S(2)}) copy-start(f32[256,256,128]{2,1,0:T(8,128)S(1)} %convert_element_type.36) | copy-start | bytes 100663296
  150.4 60.2 %copy-start.5 = (f32[2,128]{1,0:T(2,128)S(1)}, f32[2,128]{1,0:T(2,128)}, u32[]{:S(2)}) copy-start(f32[2,128]{1,0:T(2,128)} %param.8) | copy-start | bytes 3076
  212.2 36.7 %copy-start.4 = (bf16[16,256]{1,0:T(8,128)(2,1)S(1)}, bf16[16,256]{1,0:T(8,128)(2,1)}, u32[]{:S(2)}) copy-start(bf16[16,256]{1,0:T(8,128)(2,1)} %param.7) | copy-start | bytes 24580
  212.2 56.4 %copy-start.3 = (bf16[16,256,128]{2,1,0:T(8,128)(2,1)S(1)}, bf16[16,256,128]{2,1,0:T(8,128)(2,1)}, u32[]{:S(2)}) copy-start(bf16[16,256,128]{2,1,0:T(8,128)(2,1)} %param.5) | copy-start | bytes 3145732
  236.0 11.7 %copy-start.2 = (f32[2,128,256,128]{1,3,2,0:T(8,128)}, f32[2,128,256,128]{1,3,2,0:T(8,128)S(1)}, u32[]{:S(2)}) copy-start(f32[2,128,256,128]{1,3,2,0:T(8,128)S(1)} %bitcast_select_fusion) | copy-start | bytes 100663296
  248.7 97.9 %all-gather.6.cloned.1.call-start = ((), (), s32[]{:S(2)}) async-start(), calls=%async_computation.2 | async-start | bytes 8912896 | tf_op jit(solution)/shard_map/all_gather | solution.py:80
Sparse Core Ops, SparseCore 0:
  9.5 129.5 all-gather.3
  141.4 19.5 all-reduce.3
  248.8 19.7 all-reduce.5
  271.6 74.8 all-gather.5
